TPU v7x, 128 devices: a whole 4x4x4 slice. The times are simulated.
128 devices in a mesh: dev: 128 (over x, z, y, core).
Axes of the slice: x: 4, y: 4, z: 4, core: 2. Of those that a mesh axis runs over, the one named last changes fastest.
Arguments:
- source_rows: bfloat16 [131072, 4096], P('dev'), may hold values from -6 to 6
- factor: bfloat16 [8, 512, 512], replicated, may hold values from -0.25 to 0.25
- plan_start: int32 [128, 128], replicated, may hold values from 0 to 1016, as said below
- plan_count: int32 [128, 128], replicated, may hold values from 0 to 8, as said below
- partners: int32 [2, 128], replicated, may hold values from 0 to 127, as said below
Outputs:
- kernel_tiles: float32 [2, 65536, 512], P(None, 'dev')
Inputs may be any that keep to these rules, and one draw needn't show every extreme that they name: `plan_count`: entry [s, d] is how many rows source shard s sends to destination d; each column sums to exactly 512; one source's counts sum to at most 1024, and some source reaches it. `plan_start`: the row ranges of one source for the different destinations are disjoint and lie within its 1024 rows. In each round r there is one power of two m_r with partners[r, d] = d XOR m_r for every player d; the m_r of different rounds differ.
All inputs are finite; a program needn't handle non-finite values.
Results may differ from a plain program's by a relative error of at most 0.0029.
Values may be sent and summed in bfloat16 or wider, within the bound.
No kernel may reach another device: no remote copies, remote signals or barrier semaphores. Data moves between devices by JAX's collectives and lax.ppermute only.
A program may use at most 128 MiB of HBM per device.

v0:
```python
import jax
import jax.numpy as jnp
from jax import lax
from jax.sharding import PartitionSpec as P


def precondition(row_data, factor):
    block_width = factor.shape[1]
    pieces_out = []
    for layer in range(factor.shape[0]):
        pieces_out.append(
            jnp.dot(
                row_data[:, layer * block_width : (layer + 1) * block_width],
                factor[layer],
                preferred_element_type=jnp.float32,
            )
        )
    return jnp.concatenate(pieces_out, axis=1).astype(jnp.bfloat16)


def per_device(source_rows, factor, plan_start, plan_count, partners):
    devices = lax.axis_size("dev")
    own_index = lax.axis_index("dev")
    capacity, feat_width = source_rows.shape
    slot_rows = capacity // devices
    block_rows = capacity // 2
    piece_rows = block_rows // devices
    start_row = lax.dynamic_index_in_dim(plan_start, own_index, 0, keepdims=False)
    count_row = lax.dynamic_index_in_dim(plan_count, own_index, 0, keepdims=False)
    offsets = jnp.arange(slot_rows, dtype=jnp.int32)
    usable = offsets[None, :] < count_row[:, None]
    picked = jnp.where(usable, start_row[:, None] + offsets[None, :], 0).reshape(-1)
    count_col = lax.dynamic_index_in_dim(plan_count, own_index, 1, keepdims=False)
    inclusive = jnp.cumsum(count_col)
    exclusive = inclusive - count_col
    positions = jnp.arange(block_rows, dtype=jnp.int32)
    source_of = jnp.sum((inclusive[None, :] <= positions[:, None]).astype(jnp.int32), axis=1)
    source_of = jnp.minimum(source_of, devices - 1)
    one_hot = (source_of[:, None] == jnp.arange(devices, dtype=jnp.int32)[None, :]).astype(
        jnp.int32
    )
    before = jnp.sum(one_hot * exclusive[None, :], axis=1)
    arrival_index = source_of * slot_rows + positions - before
    received = lax.all_to_all(
        precondition(source_rows, factor)[picked], "dev", split_axis=0, concat_axis=0, tiled=True
    )
    blocks = received[arrival_index]
    scaling = feat_width ** (-0.5)
    tiles = []
    for round_index in range(partners.shape[0]):
        spread = lax.all_to_all(blocks, "dev", split_axis=0, concat_axis=0, tiled=True).reshape(
            devices, piece_rows, feat_width
        )
        sending = spread[partners[round_index]]
        product = jnp.einsum(
            "rf,jkf->jkr",
            blocks,
            lax.all_to_all(sending, "dev", split_axis=0, concat_axis=0, tiled=True),
            preferred_element_type=jnp.float32,
        )
        tiles.append(product.reshape(block_rows, block_rows).T * scaling)
    return jnp.stack(tiles)


def solution(mesh):
    placed = (P("dev", None), P(), P(), P(), P())
    return jax.shard_map(
        per_device, mesh=mesh, in_specs=placed, out_specs=P(None, "dev", None), check_vma=False
    )
```

profile of v0, /device:TPU:0, one launch (start us, length us, event | category | flops | bytes accessed | tf_op | source)
XLA Modules:
  0.0 389.7 jit_solution(963159984091057503)
XLA Ops:
  0.0 0.0 copy-start.2
  0.0 3.3 fusion.13
  3.3 3.1 fusion.12
  6.4 0.0 copy-start.3
  6.4 3.2 fusion.11
  9.7 0.0 copy-done.2
  9.7 2.8 fusion.10
  12.4 0.0 copy-done.3
  12.5 1.8 fusion.9
  14.2 1.7 fusion.8
  16.0 1.8 fusion.7
  17.7 1.8 fusion.6
  19.5 0.0 copy-start
  19.5 11.3 %copy.19 = bf16[1024,4096]{1,0:T(8,128)(2,1)} copy(bf16[1024,4096]{0,1:T(8,128)(2,1)} %fusion.6) | data formatting | bytes 16777216 | tf_op jit(solution)/shard_map/concatenate | solution.py:18
  30.8 0.0 copy-done
  30.8 0.7 fusion.48
  31.5 0.1 add_select_fusion
  31.6 0.1 select_n.64
  31.8 19.5 %gather_fusion = bf16[1024,4096]{1,0:T(8,128)(2,1)} fusion(bf16[1024,4096]{1,0:T(8,128)(2,1)} %copy.19, s32[1024]{0:T(1024)S(1)} %broadcast_clamp_fusion), kind=kCustom, calls=%fused_computation | custom fusion | bytes 16781312 | tf_op jit(solution)/shard_map/gather | solution.py:45
  51.3 11.9 %all-to-all-start = ((bf16[128,8,4096]{2,1,0:T(8,128)(2,1)}), bf16[128,8,4096]{2,1,0:T(8,128)(2,1)}, u32[]{:S(2)}, u32[]{:S(2)}) async-start(bf16[128,8,4096]{2,1,0:T(8,128)(2,1)} %bitcast.57), calls=%async_computation | async-start | bytes 16777216 | tf_op jit(solution)/shard_map/all_to_all | solution.py:44
  63.2 0.2 fusion.52
  63.4 0.2 reduce-window.7
  63.5 0.1 reduce
  63.7 0.2 convert_reduce_fusion
  63.8 0.2 select_reduce_fusion
  64.1 104.9 %all-to-all-done = bf16[128,8,4096]{2,1,0:T(8,128)(2,1)} async-done(((bf16[128,8,4096]{2,1,0:T(8,128)(2,1)}), bf16[128,8,4096]{2,1,0:T(8,128)(2,1)}, u32[]{:S(2)}, u32[]{:S(2)}) %all-to-all-start) | async-done | bytes 8388640 | tf_op jit(solution)/shard_map/all_to_all | solution.py:44
  169.0 13.0 %gather_fusion.1 = bf16[512,4096]{1,0:T(8,128)(2,1)} fusion(bf16[1024,4096]{1,0:T(8,128)(2,1)} %bitcast.12, s32[1024]{0:T(1024)S(1)} %pad_clamp_fusion.2), kind=kCustom, calls=%fused_computation.1 | custom fusion | bytes 8390656 | tf_op jit(solution)/shard_map/gather | solution.py:47
  182.0 7.2 %all_to_all.24 = bf16[128,4,4096]{2,1,0:T(4,128)(2,1)} reshape(bf16[512,4096]{1,0:T(8,128)(2,1)} %gather_fusion.1) | data formatting | bytes 8388608 | tf_op jit(solution)/shard_map/all_to_all | solution.py:51
  189.2 0.0 copy-start.1
  189.2 7.4 %all-to-all-start.1 = ((bf16[128,4,4096]{2,1,0:T(4,128)(2,1)}), bf16[128,4,4096]{2,1,0:T(4,128)(2,1)}, u32[]{:S(2)}, u32[]{:S(2)}) async-start(bf16[128,4,4096]{2,1,0:T(4,128)(2,1)} %all_to_all.24), calls=%async_computation.1 | async-start | bytes 8388608 | tf_op jit(solution)/shard_map/all_to_all | solution.py:51
  196.7 0.0 copy-done.1
  196.7 52.5 %all-to-all-done.1 = bf16[128,4,4096]{2,1,0:T(4,128)(2,1)} async-done(((bf16[128,4,4096]{2,1,0:T(4,128)(2,1)}), bf16[128,4,4096]{2,1,0:T(4,128)(2,1)}, u32[]{:S(2)}, u32[]{:S(2)}) %all-to-all-start.1) | async-done | bytes 4194336 | tf_op jit(solution)/shard_map/all_to_all | solution.py:51
  249.2 9.7 %gather_fusion.3 = bf16[128,4,4096]{2,1,0:T(4,128)(2,1)} fusion(bf16[128,4,4096]{2,1,0:T(4,128)(2,1)} %all-to-all-done.1, s32[1024]{0:T(1024)S(1)} %pad_clamp_fusion), kind=kCustom, calls=%fused_computation.3 | custom fusion | bytes 8389120 | tf_op jit(solution)/shard_map/gather | solution.py:54
  258.9 6.0 %all-to-all-start.3 = ((bf16[128,4,4096]{2,1,0:T(4,128)(2,1)}), bf16[128,4,4096]{2,1,0:T(4,128)(2,1)}, u32[]{:S(2)}, u32[]{:S(2)}) async-start(bf16[128,4,4096]{2,1,0:T(4,128)(2,1)} %gather_fusion.3), calls=%async_computation.3 | async-start | bytes 8388608 | tf_op jit(solution)/shard_map/all_to_all | solution.py:58
  264.9 9.7 %gather_fusion.2 = bf16[128,4,4096]{2,1,0:T(4,128)(2,1)} fusion(bf16[128,4,4096]{2,1,0:T(4,128)(2,1)} %all-to-all-done.1, s32[1024]{0:T(1024)S(1)} %pad_clamp_fusion.1), kind=kCustom, calls=%fused_computation.2 | custom fusion | bytes 8389120 | tf_op jit(solution)/shard_map/gather | solution.py:54
  274.6 42.8 %all-to-all-done.3 = bf16[128,4,4096]{2,1,0:T(4,128)(2,1)} async-done(((bf16[128,4,4096]{2,1,0:T(4,128)(2,1)}), bf16[128,4,4096]{2,1,0:T(4,128)(2,1)}, u32[]{:S(2)}, u32[]{:S(2)}) %all-to-all-start.3) | async-done | bytes 4194336 | tf_op jit(solution)/shard_map/all_to_all | solution.py:58
  317.5 6.2 %all-to-all-start.2 = ((bf16[128,4,4096]{2,1,0:T(4,128)(2,1)}), bf16[128,4,4096]{2,1,0:T(4,128)(2,1)}, u32[]{:S(2)}, u32[]{:S(2)}) async-start(bf16[128,4,4096]{2,1,0:T(4,128)(2,1)} %gather_fusion.2), calls=%async_computation.2 | async-start | bytes 8388608 | tf_op jit(solution)/shard_map/all_to_all | solution.py:58
  323.7 8.5 %fusion.19 = f32[128,4,512]{2,0,1:T(8,128)S(1)} fusion(bf16[512,4096]{1,0:T(8,128)(2,1)} %gather_fusion.1, bf16[128,4,4096]{2,1,0:T(4,128)(2,1)} %all-to-all-done.3), kind=kOutput, calls=%fused_computation.28 | convolution fusion | flops 2147745792 | bytes 9437184 | tf_op jit(solution)/shard_map/rf,jkf->jkr/dot_general | solution.py:55
  332.1 0.7 copy.23
  332.8 0.4 mul.51
  333.2 42.8 %all-to-all-done.2 = bf16[128,4,4096]{2,1,0:T(4,128)(2,1)} async-done(((bf16[128,4,4096]{2,1,0:T(4,128)(2,1)}), bf16[128,4,4096]{2,1,0:T(4,128)(2,1)}, u32[]{:S(2)}, u32[]{:S(2)}) %all-to-all-start.2) | async-done | bytes 4194336 | tf_op jit(solution)/shard_map/all_to_all | solution.py:58
  376.0 8.5 %fusion.14 = f32[128,4,512]{2,0,1:T(8,128)S(1)} fusion(bf16[512,4096]{1,0:T(8,128)(2,1)} %gather_fusion.1, bf16[128,4,4096]{2,1,0:T(4,128)(2,1)} %all-to-all-done.2), kind=kOutput, calls=%fused_computation.27 | convolution fusion | flops 2147745792 | bytes 9437184 | tf_op jit(solution)/shard_map/rf,jkf->jkr/dot_general | solution.py:55
  384.5 0.7 copy.21
  385.2 1.3 mul.48
  386.5 1.4 pad_maximum_fusion
  387.9 1.8 copy.24
  (9 shorter events, 0.1 us)
Async XLA Ops:
  0.0 9.7 %copy-start.2 = (bf16[1024,4096]{1,0:T(8,128)(2,1)S(1)}, bf16[1024,4096]{1,0:T(8,128)(2,1)}, u32[]{:S(2)}) copy-start(bf16[1024,4096]{1,0:T(8,128)(2,1)} %param.5) | copy-start | bytes 25165828
  6.4 6.0 %copy-start.3 = (bf16[8,512,512]{2,1,0:T(8,128)(2,1)S(1)}, bf16[8,512,512]{2,1,0:T(8,128)(2,1)}, u32[]{:S(2)}) copy-start(bf16[8,512,512]{2,1,0:T(8,128)(2,1)} %param.6) | copy-start | bytes 12582916
  19.5 11.3 %copy-start = (s32[128,128]{1,0:T(8,128)S(1)}, s32[128,128]{1,0:T(8,128)}, u32[]{:S(2)}) copy-start(s32[128,128]{1,0:T(8,128)} %param.8) | copy-start | bytes 196612
  51.3 117.7 %all-to-all-start = ((bf16[128,8,4096]{2,1,0:T(8,128)(2,1)}), bf16[128,8,4096]{2,1,0:T(8,128)(2,1)}, u32[]{:S(2)}, u32[]{:S(2)}) async-start(bf16[128,8,4096]{2,1,0:T(8,128)(2,1)} %bitcast.57), calls=%async_computation | async-start | bytes 16777216 | tf_op jit(solution)/shard_map/all_to_all | solution.py:44
  189.2 7.4 %copy-start.1 = (s32[2,128]{1,0:T(2,128)S(1)}, s32[2,128]{1,0:T(2,128)}, u32[]{:S(2)}) copy-start(s32[2,128]{1,0:T(2,128)} %param.9) | copy-start | bytes 3076
  189.2 60.0 %all-to-all-start.1 = ((bf16[128,4,4096]{2,1,0:T(4,128)(2,1)}), bf16[128,4,4096]{2,1,0:T(4,128)(2,1)}, u32[]{:S(2)}, u32[]{:S(2)}) async-start(bf16[128,4,4096]{2,1,0:T(4,128)(2,1)} %all_to_all.24), calls=%async_computation.1 | async-start | bytes 8388608 | tf_op jit(solution)/shard_map/all_to_all | solution.py:51
  258.9 58.5 %all-to-all-start.3 = ((bf16[128,4,4096]{2,1,0:T(4,128)(2,1)}), bf16[128,4,4096]{2,1,0:T(4,128)(2,1)}, u32[]{:S(2)}, u32[]{:S(2)}) async-start(bf16[128,4,4096]{2,1,0:T(4,128)(2,1)} %gather_fusion.3), calls=%async_computation.3 | async-start | bytes 8388608 | tf_op jit(solution)/shard_map/all_to_all | solution.py:58
  317.5 58.5 %all-to-all-start.2 = ((bf16[128,4,4096]{2,1,0:T(4,128)(2,1)}), bf16[128,4,4096]{2,1,0:T(4,128)(2,1)}, u32[]{:S(2)}, u32[]{:S(2)}) async-start(bf16[128,4,4096]{2,1,0:T(4,128)(2,1)} %gather_fusion.2), calls=%async_computation.2 | async-start | bytes 8388608 | tf_op jit(solution)/shard_map/all_to_all | solution.py:58
where the time goes:
time: 391 us; the launch traced here: 390 us
  waiting for transfers between devices  243 us (62%)
  local copies, waits for them, and re-layouts  76.4 us (20%)
  matrix products  36.5 us (9%)
  starting transfers between devices  31.4 us (8%)
    all_to_all x1, waiting for transfers between devices, per_device(): lax.all_to_all(precondition(source_rows, factor)[picked], 'dev', split_ax...  105 us
    all_to_all x2, waiting for transfers between devices, per_device(): lax.all_to_all(sending, 'dev', split_axis=0, concat_axis=0, tiled=True)  85.6 us
    all_to_all x1, waiting for transfers between devices, per_device(): lax.all_to_all(blocks, 'dev', split_axis=0, concat_axis=0, tiled=True)  52.5 us
    gather x1, local copies, waits for them, and re-layouts, per_device(): precondition(source_rows, factor)[picked]  19.5 us
    dot_general x8, matrix products, precondition(): jnp.dot(row_data[:, layer * block_width:(layer + 1) * block_width], facto...  19.5 us
    gather x2, local copies, waits for them, and re-layouts, per_device(): sending = spread[partners[round_index]]  19.4 us
    dot_general x2, matrix products, per_device(): jnp.einsum('rf,jkf->jkr', blocks, lax.all_to_all(sending, 'dev', split_ax...  17 us
    gather x1, local copies, waits for them, and re-layouts, per_device(): blocks = received[arrival_index]  13 us
  transfers between devices with their start and end apart: 4, of which 4 were waited for; matrix products, arithmetic and copies ran while one was open for 5% of the time, Pallas kernels for 0%

commit v1 on v0

v1 whole, which is shorter than its diff:
```python
import functools

import jax
import jax.numpy as jnp
from jax import lax
from jax.experimental import pallas as pl
from jax.experimental.pallas import tpu as pltpu
from jax.sharding import PartitionSpec as P

SLOT = 8
LANES = 128
MEMBERS = 4


def relative_player(device, member, masks):
    player = device
    if member & 1:
        player = player ^ masks[0]
    if member & 2:
        player = player ^ masks[1]
    return player


def role_of(device, masks):
    low = jnp.where((device & masks[0]) != 0, 1, 0)
    high = jnp.where((device & masks[1]) != 0, 2, 0)
    return low + high


def masks_of(partners_ref):
    first, second = partners_ref[0, 0], partners_ref[1, 0]
    return jnp.minimum(first, second), jnp.maximum(first, second)


def pack_kernel(me_ref, partners_ref, start_hbm, source_hbm, out_hbm, pair_ref, *scratch):
    source, wide, staged, start, got, sent, start_got = scratch
    parts, capacity, quarter = source.shape
    tiles = quarter // LANES
    takers = staged.shape[1]
    start_rows = start.shape[0]
    low, high = masks_of(partners_ref)
    row = me_ref[0] % start_rows

    def load(part):
        return pltpu.make_async_copy(
            source_hbm.at[:, pl.ds(part * quarter, quarter)], source.at[part], got.at[part]
        )

    start_load = pltpu.make_async_copy(
        start_hbm.at[pl.ds(pl.multiple_of(me_ref[0] - row, start_rows), start_rows)], start, start_got
    )
    start_load.start()
    for part in range(parts):
        load(part).start()
    pair_ref[0] = pair_index(low, high, (out_hbm.shape[0] - 1).bit_length())
    start_load.wait()

    def one_part(part, carry):
        role_bits = jnp.where((part & 1) != 0, low, 0) | jnp.where((part & 2) != 0, high, 0)

        def taker(at):
            spread = (at & (low - 1)) | ((at & ~(low - 1)) << 1)
            return (spread & (high - 1)) | ((spread & ~(high - 1)) << 1) | role_bits

        def fill(at, carry):
            device = taker(at)
            for member in range(MEMBERS):
                begin = start[row, relative_player(device, member, (low, high))]
                rows = [wide[tile, pl.ds(begin, SLOT), :] for tile in range(tiles)]
                staged[part, at, pl.ds(member * SLOT, SLOT), :] = jnp.concatenate(rows, axis=1).astype(jnp.bfloat16)
            return carry

        def send(at, carry):
            pltpu.make_async_copy(staged.at[part, at], out_hbm.at[taker(at)], sent.at[part]).start()
            return carry

        load(part).wait()
        for tile in range(tiles):
            wide[tile] = source[part, :, pl.ds(tile * LANES, LANES)].astype(jnp.float32)
        for half in range(2):
            begin, end = half * takers // 2, (half + 1) * takers // 2
            lax.fori_loop(begin, end, fill, 0, unroll=4)
            lax.fori_loop(begin, end, send, 0, unroll=4)
        return carry

    lax.fori_loop(0, parts, one_part, 0)
    for part in range(parts):
        pltpu.make_async_copy(staged.at[part], out_hbm.at[pl.ds(0, takers)], sent.at[part]).wait()


def pair_index(low, high, bits):
    low_bit = sum(jnp.where(low >= 1 << at, 1, 0) for at in range(1, bits))
    high_bit = sum(jnp.where(high >= 1 << at, 1, 0) for at in range(1, bits))
    return (low_bit * (2 * bits - 1 - low_bit)) // 2 + high_bit - low_bit - 1


def pack(source_rows, me, partners, plan_start):
    capacity, feats = source_rows.shape
    devices = plan_start.shape[0]
    quarter = feats // MEMBERS
    smem, anywhere = pl.BlockSpec(memory_space=pltpu.SMEM), pl.BlockSpec(memory_space=pl.ANY)
    return pl.pallas_call(
        pack_kernel,
        in_specs=[smem, smem, anywhere, anywhere],
        out_specs=[anywhere, smem],
        scratch_shapes=[
            pltpu.VMEM((MEMBERS, capacity, quarter), jnp.bfloat16),
            pltpu.VMEM((quarter // LANES, capacity, LANES), jnp.float32),
            pltpu.VMEM((MEMBERS, devices // MEMBERS, MEMBERS * SLOT, quarter), jnp.bfloat16),
            pltpu.SMEM((8, devices), jnp.int32),
            pltpu.SemaphoreType.DMA((MEMBERS,)),
            pltpu.SemaphoreType.DMA((MEMBERS,)),
            pltpu.SemaphoreType.DMA,
        ],
        out_shape=[
            jax.ShapeDtypeStruct((devices, MEMBERS * SLOT, quarter), jnp.bfloat16),
            jax.ShapeDtypeStruct((1,), jnp.int32),
        ],
        compiler_params=pltpu.CompilerParams(vmem_limit_bytes=56 * 1024 * 1024),
        name="pack",
    )(me, partners, plan_start, source_rows)


def partial_kernel(scale, me_ref, partners_ref, count_hbm, received_hbm, factor_hbm, *refs):
    out_hbm, (received, factor, wide, conditioned, own, lent, count, got, loaded, sent) = refs[:3], refs[3:]
    groups, group, _, quarter = received.shape
    tiles = quarter // LANES
    rows = wide.shape[2] - SLOT
    layers, width, _ = factor.shape
    each = width // LANES
    masks = masks_of(partners_ref)
    players = [relative_player(me_ref[0], member, masks) for member in range(MEMBERS)]

    def load(at):
        return pltpu.make_async_copy(received_hbm.at[pl.ds(at * group, group)], received.at[at], got.at[at])

    count_load = pltpu.make_async_copy(count_hbm, count, loaded.at[0])
    factor_load = pltpu.make_async_copy(
        factor_hbm.at[pl.ds(role_of(me_ref[0], masks) * layers, layers)], factor, loaded.at[1]
    )
    count_load.start()
    for at in range(groups):
        load(at).start()
    factor_load.start()
    count_load.wait()

    def one_group(at, begins):
        def one_source(source, begins):
            later = []
            for member in range(MEMBERS):
                run = received[at, source, pl.ds(member * SLOT, SLOT), :].astype(jnp.float32)
                for tile in range(tiles):
                    wide[member, tile, pl.ds(begins[member], SLOT), :] = run[:, tile * LANES : (tile + 1) * LANES]
                later.append(begins[member] + count[at * group + source, players[member]])
            return tuple(later)

        load(at).wait()
        return lax.fori_loop(0, group, one_source, begins, unroll=4)

    lax.fori_loop(0, groups, one_group, (jnp.int32(0),) * MEMBERS)
    factor_load.wait()
    for member in range(MEMBERS):
        for layer in range(layers):
            ordered = jnp.concatenate(
                [
                    wide[member, layer * each + tile, pl.ds(0, rows), :].astype(jnp.bfloat16)
                    for tile in range(each)
                ],
                axis=1,
            )
            conditioned[member, :, pl.ds(layer * width, width)] = jnp.dot(
                ordered, factor[layer], preferred_element_type=jnp.float32
            ).astype(jnp.bfloat16)

    def tile_of(left, right):
        return scale * lax.dot_general(
            conditioned[left],
            conditioned[right],
            (((1,), (1,)), ((), ())),
            preferred_element_type=jnp.float32,
        )

    copies = [
        pltpu.make_async_copy(own, out_hbm[0], sent.at[0]),
        pltpu.make_async_copy(lent.at[0], out_hbm[1], sent.at[1]),
        pltpu.make_async_copy(lent.at[1], out_hbm[2], sent.at[2]),
    ]
    own[0] = tile_of(0, 1)
    own[1] = tile_of(0, 2)
    lent[0] = tile_of(1, 3).astype(jnp.bfloat16)
    copies[0].start()
    lent[1] = tile_of(2, 3).astype(jnp.bfloat16)
    copies[1].start()
    copies[2].start()
    for copy in copies:
        copy.wait()


def partial_tiles(received, factor, me, partners, plan_count, scale):
    devices, slots, quarter = received.shape
    width = factor.shape[1]
    layers = quarter // width
    rows = devices * SLOT // 2
    groups = 8
    smem, anywhere = pl.BlockSpec(memory_space=pltpu.SMEM), pl.BlockSpec(memory_space=pl.ANY)
    return pl.pallas_call(
        functools.partial(partial_kernel, scale),
        in_specs=[smem, smem, anywhere, anywhere, anywhere],
        out_specs=[anywhere, anywhere, anywhere],
        scratch_shapes=[
            pltpu.VMEM((groups, devices // groups, slots, quarter), jnp.bfloat16),
            pltpu.VMEM((layers, width, width), jnp.bfloat16),
            pltpu.VMEM((MEMBERS, quarter // LANES, rows + SLOT, LANES), jnp.float32),
            pltpu.VMEM((MEMBERS, rows, quarter), jnp.bfloat16),
            pltpu.VMEM((2, rows, rows), jnp.float32),
            pltpu.VMEM((2, rows, rows), jnp.bfloat16),
            pltpu.SMEM((devices, devices), jnp.int32),
            pltpu.SemaphoreType.DMA((groups,)),
            pltpu.SemaphoreType.DMA((2,)),
            pltpu.SemaphoreType.DMA((3,)),
        ],
        out_shape=[
            jax.ShapeDtypeStruct((2, rows, rows), jnp.float32),
            jax.ShapeDtypeStruct((rows, rows), jnp.bfloat16),
            jax.ShapeDtypeStruct((rows, rows), jnp.bfloat16),
        ],
        compiler_params=pltpu.CompilerParams(vmem_limit_bytes=56 * 1024 * 1024),
        name="partial_tiles",
    )(me, partners, plan_count, received, factor)


def half_sums_kernel(own_hbm, *refs):
    added_hbm, out_hbm, (own, added, half, got, sent) = refs[:2], refs[2:4], refs[4:]
    loads = [
        [
            pltpu.make_async_copy(own_hbm.at[at], own.at[at], got.at[2 * at]),
            pltpu.make_async_copy(added_hbm[at], added.at[at], got.at[2 * at + 1]),
        ]
        for at in range(2)
    ]
    sends = [pltpu.make_async_copy(half.at[at], out_hbm[at], sent.at[at]) for at in range(2)]
    for load in loads[0] + loads[1]:
        load.start()
    for at in range(2):
        for load in loads[at]:
            load.wait()
        half[at] = (own[at] + added[at].astype(jnp.float32)).astype(jnp.bfloat16)
        sends[at].start()
    for send in sends:
        send.wait()


def half_sums(own, first, second):
    rows = own.shape[1]
    anywhere = pl.BlockSpec(memory_space=pl.ANY)
    return pl.pallas_call(
        half_sums_kernel,
        in_specs=[anywhere] * 3,
        out_specs=[anywhere] * 2,
        scratch_shapes=[
            pltpu.VMEM((2, rows, rows), jnp.float32),
            pltpu.VMEM((2, rows, rows), jnp.bfloat16),
            pltpu.VMEM((2, rows, rows), jnp.bfloat16),
            pltpu.SemaphoreType.DMA((4,)),
            pltpu.SemaphoreType.DMA((2,)),
        ],
        out_shape=[jax.ShapeDtypeStruct((rows, rows), jnp.bfloat16)] * 2,
        name="half_sums",
    )(own, first, second)


def finish_kernel(partners_ref, own_hbm, *refs):
    added_hbm, turned_hbm, out_hbm, (own, added, turned, tile, got, sent) = refs[:2], refs[2:4], refs[4], refs[5:]
    swapped = jnp.where(partners_ref[0, 0] < partners_ref[1, 0], 0, 1)
    loads = [
        [
            pltpu.make_async_copy(own_hbm.at[at], own.at[at], got.at[3 * at]),
            pltpu.make_async_copy(added_hbm[at], added.at[at], got.at[3 * at + 1]),
            pltpu.make_async_copy(turned_hbm[at], turned.at[at], got.at[3 * at + 2]),
        ]
        for at in range(2)
    ]
    sends = [pltpu.make_async_copy(tile.at[at], out_hbm.at[at ^ swapped], sent.at[at]) for at in range(2)]
    for load in loads[0] + loads[1]:
        load.start()
    for at in range(2):
        for load in loads[at]:
            load.wait()
        tile[at] = own[at] + added[at].astype(jnp.float32) + turned[at].astype(jnp.float32).T
        sends[at].start()
    for send in sends:
        send.wait()


def finish(partners, own, added, turned):
    rows = own.shape[1]
    smem, anywhere = pl.BlockSpec(memory_space=pltpu.SMEM), pl.BlockSpec(memory_space=pl.ANY)
    return pl.pallas_call(
        finish_kernel,
        in_specs=[smem, *[anywhere] * 5],
        out_specs=anywhere,
        scratch_shapes=[
            pltpu.VMEM((2, rows, rows), jnp.float32),
            pltpu.VMEM((2, rows, rows), jnp.bfloat16),
            pltpu.VMEM((2, rows, rows), jnp.bfloat16),
            pltpu.VMEM((2, rows, rows), jnp.float32),
            pltpu.SemaphoreType.DMA((6,)),
            pltpu.SemaphoreType.DMA((2,)),
        ],
        out_shape=jax.ShapeDtypeStruct((2, rows, rows), jnp.float32),
        name="finish",
    )(partners, own, *added, *turned)


def exchange(pair, devices, bits, over_low, over_high):
    def branch(low, high):
        def swap(a, b):
            return (
                lax.ppermute(a, "dev", [(at, at ^ low) for at in range(devices)]),
                lax.ppermute(b, "dev", [(at, at ^ high) for at in range(devices)]),
            )

        return swap

    branches = [branch(1 << low, 1 << high) for low in range(bits) for high in range(low + 1, bits)]
    return lax.switch(pair, branches, over_low, over_high)


def per_device(source_rows, factor, plan_start, plan_count, partners):
    devices = lax.axis_size("dev")
    bits = devices.bit_length() - 1
    me = lax.axis_index("dev").reshape(1)
    packed, pair = pack(source_rows, me, partners, plan_start)
    received = lax.all_to_all(packed, "dev", split_axis=0, concat_axis=0, tiled=True)
    received, pair = lax.optimization_barrier((received, pair))
    own, for_low, for_high = partial_tiles(received, factor, me, partners, plan_count, source_rows.shape[1] ** -0.5)
    from_low, from_high = exchange(pair[0], devices, bits, for_low, for_high)
    halves = half_sums(own, from_high, from_low)
    return finish(partners, own, (from_high, from_low), exchange(pair[0], devices, bits, *halves))


def solution(mesh):
    placed = (P("dev", None), P(), P(), P(), P())
    return jax.shard_map(
        per_device, mesh=mesh, in_specs=placed, out_specs=P(None, "dev", None), check_vma=False
    )
```

time: 391 us -> 163 us (0.42)
  waiting for transfers between devices: 243 us -> 25 us
  blocking collectives: 0 us -> 109 us
  local copies, waits for them, and re-layouts: 76.4 us -> 0 us
  matrix products: 36.5 us -> 0 us
  starting transfers between devices: 31.4 us -> 2.02 us
  Pallas kernels: 0 us -> 24.1 us
    all_to_all x4 -> x0, waiting for transfers between devices: 243 us -> none  [the longest x1 105 us: per_device(): lax.all_to_all(precondition(source_rows, factor)[picked], 'dev', split_ax...]
    all_to_all x0 -> x1, blocking collectives: none -> 109 us  [per_device(): lax.all_to_all(packed, 'dev', split_axis=0, concat_axis=0, tiled=True)]
    gather x4 -> x0, local copies, waits for them, and re-layouts: 52 us -> none  [the longest x1 19.5 us: per_device(): precondition(source_rows, factor)[picked]]
    dot_general x10 -> x0, matrix products: 36.5 us -> none  [the longest x8 19.5 us: precondition(): jnp.dot(row_data[:, layer * block_width:(layer + 1) * block_width], facto...]
    all_to_all x4 -> x0, starting transfers between devices: 31.4 us -> none  [the longest x2 12.1 us: per_device(): lax.all_to_all(sending, 'dev', split_axis=0, concat_axis=0, tiled=True)]
    ppermute x0 -> x4, waiting for transfers between devices: none -> 25 us  [the longest x2 24.1 us: swap(): lax.ppermute(a, 'dev', [(at, at ^ low) for at in range(devices)])]
    pallas_call x0 -> x4, Pallas kernels: none -> 24.1 us  [the longest x1 9.38 us: partial_tiles(): pl.pallas_call(functools.partial(partial_kernel, scale), in_specs=[smem,...]
    concatenate x1 -> x0, local copies, waits for them, and re-layouts: 11.3 us -> none  [precondition(): return jnp.concatenate(pieces_out, axis=1).astype(jnp.bfloat16)]
  transfers between devices with their start and end apart: 4 -> 4, of which waited for: 4 -> 4; matrix products, arithmetic and copies ran while one was open for 5% -> 0% of each run, Pallas kernels for 0% -> 0%
where the time goes in v1:
time: 163 us; the launch traced here: 161 us
  blocking collectives  109 us (67%)
  waiting for transfers between devices  25 us (15%)
  Pallas kernels  24.1 us (15%)
  starting transfers between devices  2.02 us (1%)
    all_to_all x1, blocking collectives, per_device(): lax.all_to_all(packed, 'dev', split_axis=0, concat_axis=0, tiled=True)  109 us
    ppermute x2, waiting for transfers between devices, swap(): lax.ppermute(a, 'dev', [(at, at ^ low) for at in range(devices)])  24.1 us
    pallas_call x1, Pallas kernels, partial_tiles(): pl.pallas_call(functools.partial(partial_kernel, scale), in_specs=[smem,...  9.38 us
    pallas_call x1, Pallas kernels, pack(): pl.pallas_call(pack_kernel, in_specs=[smem, smem, anywhere, anywhere], ou...  8.55 us
    pallas_call x1, Pallas kernels, finish(): pl.pallas_call(finish_kernel, in_specs=[smem, *[anywhere] * 5], out_specs...  4.15 us
  transfers between devices with their start and end apart: 4, of which 4 were waited for; matrix products, arithmetic and copies ran while one was open for 0% of the time, Pallas kernels for 0%

profile of v1, /device:TPU:0, one launch (start us, length us, event | category | flops | bytes accessed | tf_op | source)
XLA Modules:
  0.0 161.5 jit_solution(10478421987035956998)
XLA Ops:
  0.0 8.5 %pack.1 = (bf16[128,32,1024]{2,1,0:T(8,128)(2,1)}, s32[1]{0:T(128)}) custom-call(s32[1]{0:T(128)} %bitcast.me_ref, s32[2,128]{1,0:T(2,128)} %partners_ref.5, s32[128,128]{1,0:T(8,128)} %start_hbm.1, bf16[1024,4096]{1,0:T(8,128)(2,1)} %source_hbm.1), custom_call_target="tpu_custom_call" | custom-call | tf_op jit(solution)/shard_map/pack/pallas_call | solution.py:102
  8.6 109.5 %all_to_all.5.received_hbm = bf16[128,32,1024]{2,1,0:T(8,128)(2,1)} all-to-all(bf16[128,32,1024]{2,1,0:T(8,128)(2,1)} %get-tuple-element.268), channel_id=1, replica_groups=mesh['dev'=128] {'dev'}, dimensions={0} | all-to-all | bytes 16777216 | tf_op jit(solution)/shard_map/all_to_all | solution.py:334
  118.0 9.4 %partial_tiles.1 = (f32[2,512,512]{2,1,0:T(8,128)}, bf16[512,512]{1,0:T(8,128)(2,1)S(1)}, bf16[512,512]{1,0:T(8,128)(2,1)S(1)}) custom-call(s32[1]{0:T(128)} %bitcast.me_ref, s32[2,128]{1,0:T(2,128)} %partners_ref.5, s32[128,128]{1,0:T(8,128)} %count_hbm.1, bf16[128,32,1024]{2,1,0:T(8,128)(2,1)} %all_to_all.5.received_hbm, bf16[8,512,512]{2,1,0:T(8,128)(2,1)} %factor_hbm.1), custom_call_target="tpu_custom_call" | custom-call | tf_op jit(solution)/shard_map/partial_tiles/pallas_call | solution.py:206
  128.0 13.8 %conditional.2 = (bf16[512,512]{1,0:T(8,128)(2,1)}, bf16[512,512]{1,0:T(8,128)(2,1)}) conditional(s32[]{:T(128)} %bitcast.1, (bf16[512,512]{1,0:T(8,128)(2,1)S(1)}, bf16[512,512]{1,0:T(8,128)(2,1)S(1)}) %tuple.154, (bf16[512,512]{1,0:T(8,128)(2,1)S(1)}, bf16[512,512]{1,0:T(8,128)(2,1)S(1)}) %tuple.154, ...), branch_computations={%region_0.0_spmd, %region_1.0_spmd, %region_2.0_spmd, %region_3.0_... | conditional | bytes 4194400 | solution.py:326
  128.1 0.2 collective-permute-start.18
  128.3 0.1 collective-permute-start.19
  128.4 13.0 %collective-permute-done.18 = bf16[512,512]{1,0:T(8,128)(2,1)} collective-permute-done((bf16[512,512]{1,0:T(8,128)(2,1)S(1)}, bf16[512,512]{1,0:T(8,128)(2,1)}, u32[]{:S(2)}, u32[]{:S(2)}) %collective-permute-start.18) | collective-permute-done | bytes 524320 | tf_op jit(solution)/shard_map/cond/branch_9_fun/ppermute | solution.py:319
  141.4 0.4 collective-permute-done.19
  141.9 2.0 %half_sums.1 = (bf16[512,512]{1,0:T(8,128)(2,1)S(1)}, bf16[512,512]{1,0:T(8,128)(2,1)S(1)}) custom-call(f32[2,512,512]{2,1,0:T(8,128)} %get-tuple-element.271.own_hbm, bf16[512,512]{1,0:T(8,128)(2,1)} %get-tuple-element.275.refs_0_, bf16[512,512]{1,0:T(8,128)(2,1)} %get-tuple-element.276.refs_1_), custom_call_target="tpu_custom_call" | custom-call | tf_op jit(solution)/shard_map/half_sums/pallas_call | solution.py:256
  143.9 13.3 %conditional.3 = (bf16[512,512]{1,0:T(8,128)(2,1)}, bf16[512,512]{1,0:T(8,128)(2,1)}) conditional(s32[]{:T(128)} %bitcast.1, (bf16[512,512]{1,0:T(8,128)(2,1)S(1)}, bf16[512,512]{1,0:T(8,128)(2,1)S(1)}) %half_sums.1, (bf16[512,512]{1,0:T(8,128)(2,1)S(1)}, bf16[512,512]{1,0:T(8,128)(2,1)S(1)}) %half_sums.1, ...), branch_computations={%region_21.0_spmd, %region_22.0_spmd, %region_23.0_spmd, %region_2... | conditional | bytes 4194400 | solution.py:326
  143.9 1.4 collective-permute-start.60
  145.3 0.3 collective-permute-start.61
  145.6 11.1 %collective-permute-done.60 = bf16[512,512]{1,0:T(8,128)(2,1)} collective-permute-done((bf16[512,512]{1,0:T(8,128)(2,1)S(1)}, bf16[512,512]{1,0:T(8,128)(2,1)}, u32[]{:S(2)}, u32[]{:S(2)}) %collective-permute-start.60) | collective-permute-done | bytes 524320 | tf_op jit(solution)/shard_map/cond/branch_9_fun/ppermute | solution.py:319
  156.7 0.4 collective-permute-done.61
  157.2 4.1 %finish.1 = f32[2,512,512]{2,1,0:T(8,128)} custom-call(s32[2,128]{1,0:T(2,128)} %partners_ref.5, f32[2,512,512]{2,1,0:T(8,128)} %get-tuple-element.271.own_hbm, bf16[512,512]{1,0:T(8,128)(2,1)} %get-tuple-element.275.refs_0_, bf16[512,512]{1,0:T(8,128)(2,1)} %get-tuple-element.276.refs_1_, bf16[512,512]{1,0:T(8,128)(2,1)} %get-tuple-element.277.refs_2_, ...), custom_call_target="tpu_custom_call" | custom-call | tf_op jit(solution)/shard_map/finish/pallas_call | solution.py:298
Async XLA Ops:
  128.1 13.3 %collective-permute-start.18 = (bf16[512,512]{1,0:T(8,128)(2,1)S(1)}, bf16[512,512]{1,0:T(8,128)(2,1)}, u32[]{:S(2)}, u32[]{:S(2)}) collective-permute-start(bf16[512,512]{1,0:T(8,128)(2,1)S(1)} %get-tuple-element.191), channel_id=1, source_target_pairs={{0,2},{1,3},{2,0},{3,1},{4,6},{5,7},{6,4},{7,5},{8,10},{9,11},{10,... | collective-permute-start | bytes 1572872 | tf_op jit(solution)/shard_map/cond/branch_9_fun/ppermute | solution.py:319
  128.3 13.6 %collective-permute-start.19 = (bf16[512,512]{1,0:T(8,128)(2,1)S(1)}, bf16[512,512]{1,0:T(8,128)(2,1)}, u32[]{:S(2)}, u32[]{:S(2)}) collective-permute-start(bf16[512,512]{1,0:T(8,128)(2,1)S(1)} %get-tuple-element.192), channel_id=1, source_target_pairs={{0,32},{1,33},{2,34},{3,35},{4,36},{5,37},{6,38},{7,39},{8,40},{9,... | collective-permute-start | bytes 1572872 | tf_op jit(solution)/shard_map/cond/branch_9_fun/ppermute | solution.py:320
  143.9 12.8 %collective-permute-start.60 = (bf16[512,512]{1,0:T(8,128)(2,1)S(1)}, bf16[512,512]{1,0:T(8,128)(2,1)}, u32[]{:S(2)}, u32[]{:S(2)}) collective-permute-start(bf16[512,512]{1,0:T(8,128)(2,1)S(1)} %get-tuple-element.233), channel_id=1, source_target_pairs={{0,2},{1,3},{2,0},{3,1},{4,6},{5,7},{6,4},{7,5},{8,10},{9,11},{10,... | collective-permute-start | bytes 1572872 | tf_op jit(solution)/shard_map/cond/branch_9_fun/ppermute | solution.py:319
  145.3 11.8 %collective-permute-start.61 = (bf16[512,512]{1,0:T(8,128)(2,1)S(1)}, bf16[512,512]{1,0:T(8,128)(2,1)}, u32[]{:S(2)}, u32[]{:S(2)}) collective-permute-start(bf16[512,512]{1,0:T(8,128)(2,1)S(1)} %get-tuple-element.234), channel_id=1, source_target_pairs={{0,32},{1,33},{2,34},{3,35},{4,36},{5,37},{6,38},{7,39},{8,40},{9,... | collective-permute-start | bytes 1572872 | tf_op jit(solution)/shard_map/cond/branch_9_fun/ppermute | solution.py:320

commit v2 on v1

--- a/solution.py
+++ b/solution.py
@@ -122,7 +122,8 @@
 
 
 def partial_kernel(scale, me_ref, partners_ref, count_hbm, received_hbm, factor_hbm, *refs):
-    out_hbm, (received, factor, wide, conditioned, own, lent, count, got, loaded, sent) = refs[:3], refs[3:]
+    own, *out_hbm = refs[:3]
+    received, factor, wide, conditioned, lent, count, got, loaded, sent = refs[3:]
     groups, group, _, quarter = received.shape
     tiles = quarter // LANES
     rows = wide.shape[2] - SLOT
@@ -180,18 +181,13 @@
             preferred_element_type=jnp.float32,
         )
 
-    copies = [
-        pltpu.make_async_copy(own, out_hbm[0], sent.at[0]),
-        pltpu.make_async_copy(lent.at[0], out_hbm[1], sent.at[1]),
-        pltpu.make_async_copy(lent.at[1], out_hbm[2], sent.at[2]),
-    ]
+    copies = [pltpu.make_async_copy(lent.at[at], out_hbm[at], sent.at[at]) for at in range(2)]
+    lent[0] = tile_of(1, 3).astype(jnp.bfloat16)
+    lent[1] = tile_of(2, 3).astype(jnp.bfloat16)
+    copies[0].start()
     own[0] = tile_of(0, 1)
+    copies[1].start()
     own[1] = tile_of(0, 2)
-    lent[0] = tile_of(1, 3).astype(jnp.bfloat16)
-    copies[0].start()
-    lent[1] = tile_of(2, 3).astype(jnp.bfloat16)
-    copies[1].start()
-    copies[2].start()
     for copy in copies:
         copy.wait()
 
@@ -206,44 +202,36 @@
     return pl.pallas_call(
         functools.partial(partial_kernel, scale),
         in_specs=[smem, smem, anywhere, anywhere, anywhere],
-        out_specs=[anywhere, anywhere, anywhere],
+        out_specs=[pl.BlockSpec(memory_space=pltpu.VMEM), anywhere, anywhere],
         scratch_shapes=[
             pltpu.VMEM((groups, devices // groups, slots, quarter), jnp.bfloat16),
             pltpu.VMEM((layers, width, width), jnp.bfloat16),
             pltpu.VMEM((MEMBERS, quarter // LANES, rows + SLOT, LANES), jnp.float32),
             pltpu.VMEM((MEMBERS, rows, quarter), jnp.bfloat16),
-            pltpu.VMEM((2, rows, rows), jnp.float32),
             pltpu.VMEM((2, rows, rows), jnp.bfloat16),
             pltpu.SMEM((devices, devices), jnp.int32),
             pltpu.SemaphoreType.DMA((groups,)),
             pltpu.SemaphoreType.DMA((2,)),
-            pltpu.SemaphoreType.DMA((3,)),
+            pltpu.SemaphoreType.DMA((2,)),
         ],
         out_shape=[
-            jax.ShapeDtypeStruct((2, rows, rows), jnp.float32),
+            pltpu.VMEM((2, rows, rows), jnp.float32),
             jax.ShapeDtypeStruct((rows, rows), jnp.bfloat16),
             jax.ShapeDtypeStruct((rows, rows), jnp.bfloat16),
         ],
-        compiler_params=pltpu.CompilerParams(vmem_limit_bytes=56 * 1024 * 1024),
+        compiler_params=pltpu.CompilerParams(vmem_limit_bytes=40 * 1024 * 1024),
         name="partial_tiles",
     )(me, partners, plan_count, received, factor)
 
 
-def half_sums_kernel(own_hbm, *refs):
-    added_hbm, out_hbm, (own, added, half, got, sent) = refs[:2], refs[2:4], refs[4:]
-    loads = [
-        [
-            pltpu.make_async_copy(own_hbm.at[at], own.at[at], got.at[2 * at]),
-            pltpu.make_async_copy(added_hbm[at], added.at[at], got.at[2 * at + 1]),
-        ]
-        for at in range(2)
-    ]
+def half_sums_kernel(own, *refs):
+    added_hbm, out_hbm, (added, half, got, sent) = refs[:2], refs[2:4], refs[4:]
+    loads = [pltpu.make_async_copy(added_hbm[at], added.at[at], got.at[at]) for at in range(2)]
     sends = [pltpu.make_async_copy(half.at[at], out_hbm[at], sent.at[at]) for at in range(2)]
-    for load in loads[0] + loads[1]:
+    for load in loads:
         load.start()
     for at in range(2):
-        for load in loads[at]:
-            load.wait()
+        loads[at].wait()
         half[at] = (own[at] + added[at].astype(jnp.float32)).astype(jnp.bfloat16)
         sends[at].start()
     for send in sends:
@@ -252,31 +240,30 @@
 
 def half_sums(own, first, second):
     rows = own.shape[1]
-    anywhere = pl.BlockSpec(memory_space=pl.ANY)
+    anywhere, vmem = pl.BlockSpec(memory_space=pl.ANY), pl.BlockSpec(memory_space=pltpu.VMEM)
     return pl.pallas_call(
         half_sums_kernel,
-        in_specs=[anywhere] * 3,
-        out_specs=[anywhere] * 2,
+        in_specs=[vmem, anywhere, anywhere],
+        out_specs=[anywhere, anywhere],
         scratch_shapes=[
-            pltpu.VMEM((2, rows, rows), jnp.float32),
-            pltpu.VMEM((2, rows, rows), jnp.bfloat16),
-            pltpu.VMEM((2, rows, rows), jnp.bfloat16),
-            pltpu.SemaphoreType.DMA((4,)),
+            pltpu.VMEM((2, rows, rows), jnp.bfloat16),
+            pltpu.VMEM((2, rows, rows), jnp.bfloat16),
+            pltpu.SemaphoreType.DMA((2,)),
             pltpu.SemaphoreType.DMA((2,)),
         ],
         out_shape=[jax.ShapeDtypeStruct((rows, rows), jnp.bfloat16)] * 2,
+        compiler_params=pltpu.CompilerParams(vmem_limit_bytes=16 * 1024 * 1024),
         name="half_sums",
-    )(own, first, second)
-
-
-def finish_kernel(partners_ref, own_hbm, *refs):
-    added_hbm, turned_hbm, out_hbm, (own, added, turned, tile, got, sent) = refs[:2], refs[2:4], refs[4], refs[5:]
+    )(pltpu.with_memory_space_constraint(own, pltpu.VMEM), first, second)
+
+
+def finish_kernel(partners_ref, own, *refs):
+    added_hbm, turned_hbm, out_hbm, (added, turned, tile, got, sent) = refs[:2], refs[2:4], refs[4], refs[5:]
     swapped = jnp.where(partners_ref[0, 0] < partners_ref[1, 0], 0, 1)
     loads = [
         [
-            pltpu.make_async_copy(own_hbm.at[at], own.at[at], got.at[3 * at]),
-            pltpu.make_async_copy(added_hbm[at], added.at[at], got.at[3 * at + 1]),
-            pltpu.make_async_copy(turned_hbm[at], turned.at[at], got.at[3 * at + 2]),
+            pltpu.make_async_copy(added_hbm[at], added.at[at], got.at[2 * at]),
+            pltpu.make_async_copy(turned_hbm[at], turned.at[at], got.at[2 * at + 1]),
         ]
         for at in range(2)
     ]
@@ -297,19 +284,19 @@
     smem, anywhere = pl.BlockSpec(memory_space=pltpu.SMEM), pl.BlockSpec(memory_space=pl.ANY)
     return pl.pallas_call(
         finish_kernel,
-        in_specs=[smem, *[anywhere] * 5],
+        in_specs=[smem, pl.BlockSpec(memory_space=pltpu.VMEM), *[anywhere] * 4],
         out_specs=anywhere,
         scratch_shapes=[
+            pltpu.VMEM((2, rows, rows), jnp.bfloat16),
+            pltpu.VMEM((2, rows, rows), jnp.bfloat16),
             pltpu.VMEM((2, rows, rows), jnp.float32),
-            pltpu.VMEM((2, rows, rows), jnp.bfloat16),
-            pltpu.VMEM((2, rows, rows), jnp.bfloat16),
-            pltpu.VMEM((2, rows, rows), jnp.float32),
-            pltpu.SemaphoreType.DMA((6,)),
+            pltpu.SemaphoreType.DMA((4,)),
             pltpu.SemaphoreType.DMA((2,)),
         ],
         out_shape=jax.ShapeDtypeStruct((2, rows, rows), jnp.float32),
+        compiler_params=pltpu.CompilerParams(vmem_limit_bytes=16 * 1024 * 1024),
         name="finish",
-    )(partners, own, *added, *turned)
+    )(partners, pltpu.with_memory_space_constraint(own, pltpu.VMEM), *added, *turned)
 
 
 def exchange(pair, devices, bits, over_low, over_high):

time: 163 us -> 163 us (level)
  transfers between devices with their start and end apart: 4 -> 4, of which waited for: 4 -> 2; matrix products, arithmetic and copies ran while one was open for 0% -> 0% of each run, Pallas kernels for 0% -> 0%
where the time goes in v2:
time: 163 us; the launch traced here: 162 us
  blocking collectives  109 us (67%)
  waiting for transfers between devices  25.6 us (16%)
  Pallas kernels  22.6 us (14%)
  starting transfers between devices  3.27 us (2%)
    all_to_all x1, blocking collectives, per_device(): lax.all_to_all(packed, 'dev', split_axis=0, concat_axis=0, tiled=True)  109 us
    ppermute x2, waiting for transfers between devices, swap(): lax.ppermute(a, 'dev', [(at, at ^ low) for at in range(devices)])  25.6 us
    pallas_call x1, Pallas kernels, partial_tiles(): pl.pallas_call(functools.partial(partial_kernel, scale), in_specs=[smem,...  9.29 us
    pallas_call x1, Pallas kernels, pack(): pl.pallas_call(pack_kernel, in_specs=[smem, smem, anywhere, anywhere], ou...  8.47 us
    pallas_call x1, Pallas kernels, finish(): pl.pallas_call(finish_kernel, in_specs=[smem, pl.BlockSpec(memory_space=p...  3.42 us
  transfers between devices with their start and end apart: 4, of which 2 were waited for; matrix products, arithmetic and copies ran while one was open for 0% of the time, Pallas kernels for 0%

profile of v2, /device:TPU:0, one launch (start us, length us, event | category | flops | bytes accessed | tf_op | source)
XLA Modules:
  0.0 161.9 jit_solution(11205613190955214454)
XLA Ops:
  0.0 8.5 %pack.1 = (bf16[128,32,1024]{2,1,0:T(8,128)(2,1)}, s32[1]{0:T(128)}) custom-call(s32[1]{0:T(128)} %bitcast.me_ref, s32[2,128]{1,0:T(2,128)} %partners_ref.5, s32[128,128]{1,0:T(8,128)} %start_hbm.1, bf16[1024,4096]{1,0:T(8,128)(2,1)} %source_hbm.1), custom_call_target="tpu_custom_call" | custom-call | tf_op jit(solution)/shard_map/pack/pallas_call | solution.py:102
  8.5 0.0 copy-start
  8.5 0.0 copy-start.1
  8.5 0.0 copy-start.2
  8.5 109.5 %all_to_all.5.received_hbm = bf16[128,32,1024]{2,1,0:T(8,128)(2,1)} all-to-all(bf16[128,32,1024]{2,1,0:T(8,128)(2,1)} %get-tuple-element.268), channel_id=1, replica_groups=mesh['dev'=128] {'dev'}, dimensions={0} | all-to-all | bytes 16777216 | tf_op jit(solution)/shard_map/all_to_all | solution.py:321
  118.0 0.0 copy-done
  118.0 0.0 copy-done.1
  118.0 0.0 copy-done.2
  118.0 9.3 %partial_tiles.1 = (f32[2,512,512]{2,1,0:T(8,128)S(1)}, bf16[512,512]{1,0:T(8,128)(2,1)S(1)}, bf16[512,512]{1,0:T(8,128)(2,1)S(1)}) custom-call(s32[1]{0:T(128)} %bitcast.me_ref, s32[2,128]{1,0:T(2,128)S(1)} %copy-done.2, s32[128,128]{1,0:T(8,128)S(1)} %copy-done.1, bf16[128,32,1024]{2,1,0:T(8,128)(2,1)} %all_to_all.5.received_hbm, ...), custom_call_target="tpu_custom_call" | custom-call | tf_op jit(solution)/shard_map/partial_tiles/pallas_call | solution.py:202
  128.0 14.9 %conditional.2 = (bf16[512,512]{1,0:T(8,128)(2,1)}, bf16[512,512]{1,0:T(8,128)(2,1)}) conditional(s32[]{:T(128)} %bitcast.1, (bf16[512,512]{1,0:T(8,128)(2,1)S(1)}, bf16[512,512]{1,0:T(8,128)(2,1)S(1)}) %tuple.154, (bf16[512,512]{1,0:T(8,128)(2,1)S(1)}, bf16[512,512]{1,0:T(8,128)(2,1)S(1)}) %tuple.154, ...), branch_computations={%region_0.0_spmd, %region_1.0_spmd, %region_2.0_spmd, %region_3.0_... | conditional | bytes 4194400 | solution.py:313
  128.0 1.2 collective-permute-start.26
  129.1 0.0 collective-permute-start.27
  129.1 13.7 %collective-permute-done.26 = bf16[512,512]{1,0:T(8,128)(2,1)} collective-permute-done((bf16[512,512]{1,0:T(8,128)(2,1)S(1)}, bf16[512,512]{1,0:T(8,128)(2,1)}, u32[]{:S(2)}, u32[]{:S(2)}) %collective-permute-start.26) | collective-permute-done | bytes 524320 | tf_op jit(solution)/shard_map/cond/branch_13_fun/ppermute | solution.py:306
  142.8 0.0 collective-permute-done.27
  142.8 1.4 half_sums.1
  144.2 14.0 %conditional.3 = (bf16[512,512]{1,0:T(8,128)(2,1)}, bf16[512,512]{1,0:T(8,128)(2,1)}) conditional(s32[]{:T(128)} %bitcast.1, (bf16[512,512]{1,0:T(8,128)(2,1)S(1)}, bf16[512,512]{1,0:T(8,128)(2,1)S(1)}) %half_sums.1, (bf16[512,512]{1,0:T(8,128)(2,1)S(1)}, bf16[512,512]{1,0:T(8,128)(2,1)S(1)}) %half_sums.1, ...), branch_computations={%region_21.0_spmd, %region_22.0_spmd, %region_23.0_spmd, %region_2... | conditional | bytes 4194400 | solution.py:313
  144.3 1.8 %collective-permute-start.68 = (bf16[512,512]{1,0:T(8,128)(2,1)S(1)}, bf16[512,512]{1,0:T(8,128)(2,1)}, u32[]{:S(2)}, u32[]{:S(2)}) collective-permute-start(bf16[512,512]{1,0:T(8,128)(2,1)S(1)} %get-tuple-element.241), channel_id=1, source_target_pairs={{0,4},{1,5},{2,6},{3,7},{4,0},{5,1},{6,2},{7,3},{8,12},{9,13},{10,... | collective-permute-start | bytes 1572872 | tf_op jit(solution)/shard_map/cond/branch_13_fun/ppermute | solution.py:306
  146.1 0.3 collective-permute-start.69
  146.4 11.9 %collective-permute-done.68 = bf16[512,512]{1,0:T(8,128)(2,1)} collective-permute-done((bf16[512,512]{1,0:T(8,128)(2,1)S(1)}, bf16[512,512]{1,0:T(8,128)(2,1)}, u32[]{:S(2)}, u32[]{:S(2)}) %collective-permute-start.68) | collective-permute-done | bytes 524320 | tf_op jit(solution)/shard_map/cond/branch_13_fun/ppermute | solution.py:306
  158.3 0.0 collective-permute-done.69
  158.3 3.4 %finish.1 = f32[2,512,512]{2,1,0:T(8,128)} custom-call(s32[2,128]{1,0:T(2,128)S(1)} %copy-done.2, f32[2,512,512]{2,1,0:T(8,128)S(1)} %get-tuple-element.271.own, bf16[512,512]{1,0:T(8,128)(2,1)} %get-tuple-element.275.refs_0_, bf16[512,512]{1,0:T(8,128)(2,1)} %get-tuple-element.276.refs_1_, bf16[512,512]{1,0:T(8,128)(2,1)} %get-tuple-element.277.refs_2_, ...), custom_call_target="tpu_custom_call" | custom-call | tf_op jit(solution)/shard_map/finish/pallas_call | solution.py:285
Async XLA Ops:
  8.5 109.5 %copy-start = (bf16[8,512,512]{2,1,0:T(8,128)(2,1)S(1)}, bf16[8,512,512]{2,1,0:T(8,128)(2,1)}, u32[]{:S(2)}) copy-start(bf16[8,512,512]{2,1,0:T(8,128)(2,1)} %factor_hbm.1) | copy-start | bytes 12582916
  8.5 109.5 %copy-start.1 = (s32[128,128]{1,0:T(8,128)S(1)}, s32[128,128]{1,0:T(8,128)}, u32[]{:S(2)}) copy-start(s32[128,128]{1,0:T(8,128)} %count_hbm.1) | copy-start | bytes 196612
  8.5 109.5 %copy-start.2 = (s32[2,128]{1,0:T(2,128)S(1)}, s32[2,128]{1,0:T(2,128)}, u32[]{:S(2)}) copy-start(s32[2,128]{1,0:T(2,128)} %partners_ref.5) | copy-start | bytes 3076
  128.0 14.9 %collective-permute-start.26 = (bf16[512,512]{1,0:T(8,128)(2,1)S(1)}, bf16[512,512]{1,0:T(8,128)(2,1)}, u32[]{:S(2)}, u32[]{:S(2)}) collective-permute-start(bf16[512,512]{1,0:T(8,128)(2,1)S(1)} %get-tuple-element.199), channel_id=1, source_target_pairs={{0,4},{1,5},{2,6},{3,7},{4,0},{5,1},{6,2},{7,3},{8,12},{9,13},{10,... | collective-permute-start | bytes 1572872 | tf_op jit(solution)/shard_map/cond/branch_13_fun/ppermute | solution.py:306
  129.1 13.7 %collective-permute-start.27 = (bf16[512,512]{1,0:T(8,128)(2,1)S(1)}, bf16[512,512]{1,0:T(8,128)(2,1)}, u32[]{:S(2)}, u32[]{:S(2)}) collective-permute-start(bf16[512,512]{1,0:T(8,128)(2,1)S(1)} %get-tuple-element.200), channel_id=1, source_target_pairs={{0,32},{1,33},{2,34},{3,35},{4,36},{5,37},{6,38},{7,39},{8,40},{9,... | collective-permute-start | bytes 1572872 | tf_op jit(solution)/shard_map/cond/branch_13_fun/ppermute | solution.py:307
  144.3 14.0 %collective-permute-start.68 = (bf16[512,512]{1,0:T(8,128)(2,1)S(1)}, bf16[512,512]{1,0:T(8,128)(2,1)}, u32[]{:S(2)}, u32[]{:S(2)}) collective-permute-start(bf16[512,512]{1,0:T(8,128)(2,1)S(1)} %get-tuple-element.241), channel_id=1, source_target_pairs={{0,4},{1,5},{2,6},{3,7},{4,0},{5,1},{6,2},{7,3},{8,12},{9,13},{10,... | collective-permute-start | bytes 1572872 | tf_op jit(solution)/shard_map/cond/branch_13_fun/ppermute | solution.py:306
  146.1 12.2 %collective-permute-start.69 = (bf16[512,512]{1,0:T(8,128)(2,1)S(1)}, bf16[512,512]{1,0:T(8,128)(2,1)}, u32[]{:S(2)}, u32[]{:S(2)}) collective-permute-start(bf16[512,512]{1,0:T(8,128)(2,1)S(1)} %get-tuple-element.242), channel_id=1, source_target_pairs={{0,32},{1,33},{2,34},{3,35},{4,36},{5,37},{6,38},{7,39},{8,40},{9,... | collective-permute-start | bytes 1572872 | tf_op jit(solution)/shard_map/cond/branch_13_fun/ppermute | solution.py:307

commit v3 on v2

--- a/solution.py
+++ b/solution.py
@@ -10,6 +10,11 @@
 SLOT = 8
 LANES = 128
 MEMBERS = 4
+RING_BITS = 0b0101010
+
+
+def shares_ring(low, high):
+    return ((low & RING_BITS) != 0) & (high == 2 * low)
 
 
 def relative_player(device, member, masks):
@@ -183,7 +188,8 @@
 
     copies = [pltpu.make_async_copy(lent.at[at], out_hbm[at], sent.at[at]) for at in range(2)]
     lent[0] = tile_of(1, 3).astype(jnp.bfloat16)
-    lent[1] = tile_of(2, 3).astype(jnp.bfloat16)
+    turn = jnp.where(shares_ring(*masks), 1, 0)
+    lent[1] = tile_of(2 + turn, 3 - turn).astype(jnp.bfloat16)
     copies[0].start()
     own[0] = tile_of(0, 1)
     copies[1].start()
@@ -299,8 +305,11 @@
     )(partners, pltpu.with_memory_space_constraint(own, pltpu.VMEM), *added, *turned)
 
 
-def exchange(pair, devices, bits, over_low, over_high):
+def exchange(pair, devices, bits, over_low, over_high, first):
     def branch(low, high):
+        if first and shares_ring(low, high):
+            high = low ^ high
+
         def swap(a, b):
             return (
                 lax.ppermute(a, "dev", [(at, at ^ low) for at in range(devices)]),
@@ -321,9 +330,9 @@
     received = lax.all_to_all(packed, "dev", split_axis=0, concat_axis=0, tiled=True)
     received, pair = lax.optimization_barrier((received, pair))
     own, for_low, for_high = partial_tiles(received, factor, me, partners, plan_count, source_rows.shape[1] ** -0.5)
-    from_low, from_high = exchange(pair[0], devices, bits, for_low, for_high)
+    from_low, from_high = exchange(pair[0], devices, bits, for_low, for_high, True)
     halves = half_sums(own, from_high, from_low)
-    return finish(partners, own, (from_high, from_low), exchange(pair[0], devices, bits, *halves))
+    return finish(partners, own, (from_high, from_low), exchange(pair[0], devices, bits, *halves, False))
 
 
 def solution(mesh):

time: 163 us -> 164 us (level); the launches traced: 162 us -> 165 us
  waiting for transfers between devices: 25.6 us -> 28.2 us
    ppermute x2, waiting for transfers between devices: 0.01 us -> 27.8 us  [swap(): lax.ppermute(b, 'dev', [(at, at ^ high) for at in range(devices)])]
    ppermute x2, waiting for transfers between devices: 25.6 us -> 0.42 us  [swap(): lax.ppermute(a, 'dev', [(at, at ^ low) for at in range(devices)])]
    ppermute x2, starting transfers between devices: 0.29 us -> 3.63 us  [swap(): lax.ppermute(b, 'dev', [(at, at ^ high) for at in range(devices)])]
    ppermute x2, starting transfers between devices: 2.98 us -> 0.17 us  [swap(): lax.ppermute(a, 'dev', [(at, at ^ low) for at in range(devices)])]
  transfers between devices with their start and end apart: 4 -> 4, of which waited for: 2 -> 4; matrix products, arithmetic and copies ran while one was open for 0% -> 0% of each run, Pallas kernels for 0% -> 0%
where the time goes in v3:
time: 164 us; the launch traced here: 165 us
  blocking collectives  109 us (66%)
  waiting for transfers between devices  28.2 us (17%)
  Pallas kernels  22.7 us (14%)
  starting transfers between devices  3.81 us (2%)
    all_to_all x1, blocking collectives, per_device(): lax.all_to_all(packed, 'dev', split_axis=0, concat_axis=0, tiled=True)  109 us
    ppermute x2, waiting for transfers between devices, swap(): lax.ppermute(b, 'dev', [(at, at ^ high) for at in range(devices)])  27.8 us
    pallas_call x1, Pallas kernels, partial_tiles(): pl.pallas_call(functools.partial(partial_kernel, scale), in_specs=[smem,...  9.29 us
    pallas_call x1, Pallas kernels, pack(): pl.pallas_call(pack_kernel, in_specs=[smem, smem, anywhere, anywhere], ou...  8.56 us
    ppermute x2, starting transfers between devices, swap(): lax.ppermute(b, 'dev', [(at, at ^ high) for at in range(devices)])  3.63 us
    pallas_call x1, Pallas kernels, finish(): pl.pallas_call(finish_kernel, in_specs=[smem, pl.BlockSpec(memory_space=p...  3.41 us
  transfers between devices with their start and end apart: 4, of which 4 were waited for; matrix products, arithmetic and copies ran while one was open for 0% of the time, Pallas kernels for 0%

profile of v3, /device:TPU:0, one launch (start us, length us, event | category | flops | bytes accessed | tf_op | source)
XLA Modules:
  0.0 165.1 jit_solution(6792141653177178008)
XLA Ops:
  0.0 8.6 %pack.1 = (bf16[128,32,1024]{2,1,0:T(8,128)(2,1)}, s32[1]{0:T(128)}) custom-call(s32[1]{0:T(128)} %bitcast.me_ref, s32[2,128]{1,0:T(2,128)} %partners_ref.5, s32[128,128]{1,0:T(8,128)} %start_hbm.1, bf16[1024,4096]{1,0:T(8,128)(2,1)} %source_hbm.1), custom_call_target="tpu_custom_call" | custom-call | tf_op jit(solution)/shard_map/pack/pallas_call | solution.py:107
  8.6 0.0 copy-start
  8.6 0.0 copy-start.1
  8.6 0.0 copy-start.2
  8.6 109.5 %all_to_all.5.received_hbm = bf16[128,32,1024]{2,1,0:T(8,128)(2,1)} all-to-all(bf16[128,32,1024]{2,1,0:T(8,128)(2,1)} %get-tuple-element.268), channel_id=1, replica_groups=mesh['dev'=128] {'dev'}, dimensions={0} | all-to-all | bytes 16777216 | tf_op jit(solution)/shard_map/all_to_all | solution.py:330
  118.1 0.0 copy-done
  118.1 0.0 copy-done.1
  118.1 0.0 copy-done.2
  118.1 9.3 %partial_tiles.1 = (f32[2,512,512]{2,1,0:T(8,128)S(1)}, bf16[512,512]{1,0:T(8,128)(2,1)S(1)}, bf16[512,512]{1,0:T(8,128)(2,1)S(1)}) custom-call(s32[1]{0:T(128)} %bitcast.me_ref, s32[2,128]{1,0:T(2,128)S(1)} %copy-done.2, s32[128,128]{1,0:T(8,128)S(1)} %copy-done.1, bf16[128,32,1024]{2,1,0:T(8,128)(2,1)} %all_to_all.5.received_hbm, ...), custom_call_target="tpu_custom_call" | custom-call | tf_op jit(solution)/shard_map/partial_tiles/pallas_call | solution.py:208
  128.0 16.1 %conditional.2 = (bf16[512,512]{1,0:T(8,128)(2,1)}, bf16[512,512]{1,0:T(8,128)(2,1)}) conditional(s32[]{:T(128)} %bitcast.1, (bf16[512,512]{1,0:T(8,128)(2,1)S(1)}, bf16[512,512]{1,0:T(8,128)(2,1)S(1)}) %tuple.154, (bf16[512,512]{1,0:T(8,128)(2,1)S(1)}, bf16[512,512]{1,0:T(8,128)(2,1)S(1)}) %tuple.154, ...), branch_computations={%region_0.0_spmd, %region_1.0_spmd, %region_2.0_spmd, %region_3.0_... | conditional | bytes 4194400 | solution.py:322
  128.1 0.1 collective-permute-start.10
  128.2 1.8 %collective-permute-start.11 = (bf16[512,512]{1,0:T(8,128)(2,1)S(1)}, bf16[512,512]{1,0:T(8,128)(2,1)}, u32[]{:S(2)}, u32[]{:S(2)}) collective-permute-start(bf16[512,512]{1,0:T(8,128)(2,1)S(1)} %get-tuple-element.184), channel_id=1, source_target_pairs={{0,64},{1,65},{2,66},{3,67},{4,68},{5,69},{6,70},{7,71},{8,72},{9,... | collective-permute-start | bytes 1572872 | tf_op jit(solution)/shard_map/cond/branch_5_fun/ppermute | solution.py:316
  130.0 0.2 collective-permute-done.10
  130.2 13.9 %collective-permute-done.11 = bf16[512,512]{1,0:T(8,128)(2,1)} collective-permute-done((bf16[512,512]{1,0:T(8,128)(2,1)S(1)}, bf16[512,512]{1,0:T(8,128)(2,1)}, u32[]{:S(2)}, u32[]{:S(2)}) %collective-permute-start.11) | collective-permute-done | bytes 524320 | tf_op jit(solution)/shard_map/cond/branch_5_fun/ppermute | solution.py:316
  144.1 1.4 half_sums.1
  145.5 16.1 %conditional.3 = (bf16[512,512]{1,0:T(8,128)(2,1)}, bf16[512,512]{1,0:T(8,128)(2,1)}) conditional(s32[]{:T(128)} %bitcast.1, (bf16[512,512]{1,0:T(8,128)(2,1)S(1)}, bf16[512,512]{1,0:T(8,128)(2,1)S(1)}) %half_sums.1, (bf16[512,512]{1,0:T(8,128)(2,1)S(1)}, bf16[512,512]{1,0:T(8,128)(2,1)S(1)}) %half_sums.1, ...), branch_computations={%region_21.0_spmd, %region_22.0_spmd, %region_23.0_spmd, %region_2... | conditional | bytes 4194400 | solution.py:322
  145.5 0.1 collective-permute-start.52
  145.6 1.8 %collective-permute-start.53 = (bf16[512,512]{1,0:T(8,128)(2,1)S(1)}, bf16[512,512]{1,0:T(8,128)(2,1)}, u32[]{:S(2)}, u32[]{:S(2)}) collective-permute-start(bf16[512,512]{1,0:T(8,128)(2,1)S(1)} %get-tuple-element.226), channel_id=1, source_target_pairs={{0,64},{1,65},{2,66},{3,67},{4,68},{5,69},{6,70},{7,71},{8,72},{9,... | collective-permute-start | bytes 1572872 | tf_op jit(solution)/shard_map/cond/branch_5_fun/ppermute | solution.py:316
  147.4 0.2 collective-permute-done.52
  147.6 13.9 %collective-permute-done.53 = bf16[512,512]{1,0:T(8,128)(2,1)} collective-permute-done((bf16[512,512]{1,0:T(8,128)(2,1)S(1)}, bf16[512,512]{1,0:T(8,128)(2,1)}, u32[]{:S(2)}, u32[]{:S(2)}) %collective-permute-start.53) | collective-permute-done | bytes 524320 | tf_op jit(solution)/shard_map/cond/branch_5_fun/ppermute | solution.py:316
  161.5 3.4 %finish.1 = f32[2,512,512]{2,1,0:T(8,128)} custom-call(s32[2,128]{1,0:T(2,128)S(1)} %copy-done.2, f32[2,512,512]{2,1,0:T(8,128)S(1)} %get-tuple-element.271.own, bf16[512,512]{1,0:T(8,128)(2,1)} %get-tuple-element.275.refs_0_, bf16[512,512]{1,0:T(8,128)(2,1)} %get-tuple-element.276.refs_1_, bf16[512,512]{1,0:T(8,128)(2,1)} %get-tuple-element.277.refs_2_, ...), custom_call_target="tpu_custom_call" | custom-call | tf_op jit(solution)/shard_map/finish/pallas_call | solution.py:291
Async XLA Ops:
  8.6 109.5 %copy-start = (bf16[8,512,512]{2,1,0:T(8,128)(2,1)S(1)}, bf16[8,512,512]{2,1,0:T(8,128)(2,1)}, u32[]{:S(2)}) copy-start(bf16[8,512,512]{2,1,0:T(8,128)(2,1)} %factor_hbm.1) | copy-start | bytes 12582916
  8.6 109.5 %copy-start.1 = (s32[128,128]{1,0:T(8,128)S(1)}, s32[128,128]{1,0:T(8,128)}, u32[]{:S(2)}) copy-start(s32[128,128]{1,0:T(8,128)} %count_hbm.1) | copy-start | bytes 196612
  8.6 109.5 %copy-start.2 = (s32[2,128]{1,0:T(2,128)S(1)}, s32[2,128]{1,0:T(2,128)}, u32[]{:S(2)}) copy-start(s32[2,128]{1,0:T(2,128)} %partners_ref.5) | copy-start | bytes 3076
  128.1 2.1 %collective-permute-start.10 = (bf16[512,512]{1,0:T(8,128)(2,1)S(1)}, bf16[512,512]{1,0:T(8,128)(2,1)}, u32[]{:S(2)}, u32[]{:S(2)}) collective-permute-start(bf16[512,512]{1,0:T(8,128)(2,1)S(1)} %get-tuple-element.183), channel_id=1, source_target_pairs={{0,1},{1,0},{2,3},{3,2},{4,5},{5,4},{6,7},{7,6},{8,9},{9,8},{10,11... | collective-permute-start | bytes 1572872 | tf_op jit(solution)/shard_map/cond/branch_5_fun/ppermute | solution.py:315
  128.2 15.9 %collective-permute-start.11 = (bf16[512,512]{1,0:T(8,128)(2,1)S(1)}, bf16[512,512]{1,0:T(8,128)(2,1)}, u32[]{:S(2)}, u32[]{:S(2)}) collective-permute-start(bf16[512,512]{1,0:T(8,128)(2,1)S(1)} %get-tuple-element.184), channel_id=1, source_target_pairs={{0,64},{1,65},{2,66},{3,67},{4,68},{5,69},{6,70},{7,71},{8,72},{9,... | collective-permute-start | bytes 1572872 | tf_op jit(solution)/shard_map/cond/branch_5_fun/ppermute | solution.py:316
  145.5 2.1 %collective-permute-start.52 = (bf16[512,512]{1,0:T(8,128)(2,1)S(1)}, bf16[512,512]{1,0:T(8,128)(2,1)}, u32[]{:S(2)}, u32[]{:S(2)}) collective-permute-start(bf16[512,512]{1,0:T(8,128)(2,1)S(1)} %get-tuple-element.225), channel_id=1, source_target_pairs={{0,1},{1,0},{2,3},{3,2},{4,5},{5,4},{6,7},{7,6},{8,9},{9,8},{10,11... | collective-permute-start | bytes 1572872 | tf_op jit(solution)/shard_map/cond/branch_5_fun/ppermute | solution.py:315
  145.6 15.9 %collective-permute-start.53 = (bf16[512,512]{1,0:T(8,128)(2,1)S(1)}, bf16[512,512]{1,0:T(8,128)(2,1)}, u32[]{:S(2)}, u32[]{:S(2)}) collective-permute-start(bf16[512,512]{1,0:T(8,128)(2,1)S(1)} %get-tuple-element.226), channel_id=1, source_target_pairs={{0,64},{1,65},{2,66},{3,67},{4,68},{5,69},{6,70},{7,71},{8,72},{9,... | collective-permute-start | bytes 1572872 | tf_op jit(solution)/shard_map/cond/branch_5_fun/ppermute | solution.py:316

commit v4 on v3

--- a/solution.py
+++ b/solution.py
@@ -37,11 +37,11 @@
     return jnp.minimum(first, second), jnp.maximum(first, second)
 
 
-def pack_kernel(me_ref, partners_ref, start_hbm, source_hbm, out_hbm, pair_ref, *scratch):
-    source, wide, staged, start, got, sent, start_got = scratch
+def pack_kernel(me_ref, partners_ref, start_hbm, source_hbm, out_ref, pair_ref, *scratch):
+    source, wide, start, got, start_got = scratch
     parts, capacity, quarter = source.shape
     tiles = quarter // LANES
-    takers = staged.shape[1]
+    takers = out_ref.shape[0] // parts
     start_rows = start.shape[0]
     low, high = masks_of(partners_ref)
     row = me_ref[0] % start_rows
@@ -57,7 +57,7 @@
     start_load.start()
     for part in range(parts):
         load(part).start()
-    pair_ref[0] = pair_index(low, high, (out_hbm.shape[0] - 1).bit_length())
+    pair_ref[0] = pair_index(low, high, (out_ref.shape[0] - 1).bit_length())
     start_load.wait()
 
     def one_part(part, carry):
@@ -72,25 +72,15 @@
             for member in range(MEMBERS):
                 begin = start[row, relative_player(device, member, (low, high))]
                 rows = [wide[tile, pl.ds(begin, SLOT), :] for tile in range(tiles)]
-                staged[part, at, pl.ds(member * SLOT, SLOT), :] = jnp.concatenate(rows, axis=1).astype(jnp.bfloat16)
-            return carry
-
-        def send(at, carry):
-            pltpu.make_async_copy(staged.at[part, at], out_hbm.at[taker(at)], sent.at[part]).start()
+                out_ref[device, pl.ds(member * SLOT, SLOT), :] = jnp.concatenate(rows, axis=1).astype(jnp.bfloat16)
             return carry
 
         load(part).wait()
         for tile in range(tiles):
             wide[tile] = source[part, :, pl.ds(tile * LANES, LANES)].astype(jnp.float32)
-        for half in range(2):
-            begin, end = half * takers // 2, (half + 1) * takers // 2
-            lax.fori_loop(begin, end, fill, 0, unroll=4)
-            lax.fori_loop(begin, end, send, 0, unroll=4)
-        return carry
+        return lax.fori_loop(0, takers, fill, carry, unroll=8)
 
     lax.fori_loop(0, parts, one_part, 0)
-    for part in range(parts):
-        pltpu.make_async_copy(staged.at[part], out_hbm.at[pl.ds(0, takers)], sent.at[part]).wait()
 
 
 def pair_index(low, high, bits):
@@ -107,21 +97,19 @@
     return pl.pallas_call(
         pack_kernel,
         in_specs=[smem, smem, anywhere, anywhere],
-        out_specs=[anywhere, smem],
+        out_specs=[pl.BlockSpec(memory_space=pltpu.VMEM), smem],
         scratch_shapes=[
             pltpu.VMEM((MEMBERS, capacity, quarter), jnp.bfloat16),
             pltpu.VMEM((quarter // LANES, capacity, LANES), jnp.float32),
-            pltpu.VMEM((MEMBERS, devices // MEMBERS, MEMBERS * SLOT, quarter), jnp.bfloat16),
             pltpu.SMEM((8, devices), jnp.int32),
             pltpu.SemaphoreType.DMA((MEMBERS,)),
-            pltpu.SemaphoreType.DMA((MEMBERS,)),
             pltpu.SemaphoreType.DMA,
         ],
         out_shape=[
-            jax.ShapeDtypeStruct((devices, MEMBERS * SLOT, quarter), jnp.bfloat16),
+            pltpu.VMEM((devices, MEMBERS * SLOT, quarter), jnp.bfloat16),
             jax.ShapeDtypeStruct((1,), jnp.int32),
         ],
-        compiler_params=pltpu.CompilerParams(vmem_limit_bytes=56 * 1024 * 1024),
+        compiler_params=pltpu.CompilerParams(vmem_limit_bytes=52 * 1024 * 1024),
         name="pack",
     )(me, partners, plan_start, source_rows)
 

time: 164 us -> 165 us (level); the launches traced: 165 us -> 164 us
  no operation moved by 1% of the time
where the time goes in v4:
time: 165 us; the launch traced here: 164 us
  blocking collectives  109 us (66%)
  waiting for transfers between devices  29.7 us (18%)
  Pallas kernels  22.1 us (13%)
  starting transfers between devices  2.39 us (1%)
    all_to_all x1, blocking collectives, per_device(): lax.all_to_all(packed, 'dev', split_axis=0, concat_axis=0, tiled=True)  109 us
    ppermute x2, waiting for transfers between devices, swap(): lax.ppermute(b, 'dev', [(at, at ^ high) for at in range(devices)])  27.8 us
    pallas_call x1, Pallas kernels, partial_tiles(): pl.pallas_call(functools.partial(partial_kernel, scale), in_specs=[smem,...  9.3 us
    pallas_call x1, Pallas kernels, pack(): pl.pallas_call(pack_kernel, in_specs=[smem, smem, anywhere, anywhere], ou...  8 us
    pallas_call x1, Pallas kernels, finish(): pl.pallas_call(finish_kernel, in_specs=[smem, pl.BlockSpec(memory_space=p...  3.4 us
  transfers between devices with their start and end apart: 4, of which 4 were waited for; matrix products, arithmetic and copies ran while one was open for 0% of the time, Pallas kernels for 0%

profile of v4, /device:TPU:0, one launch (start us, length us, event | category | flops | bytes accessed | tf_op | source)
XLA Modules:
  0.0 164.4 jit_solution(10480596536898988702)
XLA Ops:
  0.0 8.0 %pack.1 = (bf16[128,32,1024]{2,1,0:T(8,128)(2,1)S(1)}, s32[1]{0:T(128)}) custom-call(s32[1]{0:T(128)} %bitcast.me_ref, s32[2,128]{1,0:T(2,128)} %partners_ref.5, s32[128,128]{1,0:T(8,128)} %start_hbm.1, bf16[1024,4096]{1,0:T(8,128)(2,1)} %source_hbm.1), custom_call_target="tpu_custom_call" | custom-call | tf_op jit(solution)/shard_map/pack/pallas_call | solution.py:97
  8.0 0.0 copy-start
  8.0 0.0 copy-start.1
  8.0 0.0 copy-start.2
  8.0 109.3 %all_to_all.5.received_hbm = bf16[128,32,1024]{2,1,0:T(8,128)(2,1)} all-to-all(bf16[128,32,1024]{2,1,0:T(8,128)(2,1)S(1)} %get-tuple-element.268), channel_id=1, replica_groups=mesh['dev'=128] {'dev'}, dimensions={0} | all-to-all | bytes 16777216 | tf_op jit(solution)/shard_map/all_to_all | solution.py:318
  117.3 0.0 copy-done
  117.3 0.0 copy-done.1
  117.3 0.0 copy-done.2
  117.3 9.3 %partial_tiles.1 = (f32[2,512,512]{2,1,0:T(8,128)S(1)}, bf16[512,512]{1,0:T(8,128)(2,1)S(1)}, bf16[512,512]{1,0:T(8,128)(2,1)S(1)}) custom-call(s32[1]{0:T(128)} %bitcast.me_ref, s32[2,128]{1,0:T(2,128)S(1)} %copy-done.2, s32[128,128]{1,0:T(8,128)S(1)} %copy-done.1, bf16[128,32,1024]{2,1,0:T(8,128)(2,1)} %all_to_all.5.received_hbm, ...), custom_call_target="tpu_custom_call" | custom-call | tf_op jit(solution)/shard_map/partial_tiles/pallas_call | solution.py:196
  127.3 16.1 %conditional.2 = (bf16[512,512]{1,0:T(8,128)(2,1)}, bf16[512,512]{1,0:T(8,128)(2,1)}) conditional(s32[]{:T(128)} %bitcast.1, (bf16[512,512]{1,0:T(8,128)(2,1)S(1)}, bf16[512,512]{1,0:T(8,128)(2,1)S(1)}) %tuple.154, (bf16[512,512]{1,0:T(8,128)(2,1)S(1)}, bf16[512,512]{1,0:T(8,128)(2,1)S(1)}) %tuple.154, ...), branch_computations={%region_0.0_spmd, %region_1.0_spmd, %region_2.0_spmd, %region_3.0_... | conditional | bytes 4194400 | solution.py:310
  127.4 0.1 collective-permute-start.6
  127.5 1.1 collective-permute-start.7
  128.6 0.9 collective-permute-done.6
  129.5 13.9 %collective-permute-done.7 = bf16[512,512]{1,0:T(8,128)(2,1)} collective-permute-done((bf16[512,512]{1,0:T(8,128)(2,1)S(1)}, bf16[512,512]{1,0:T(8,128)(2,1)}, u32[]{:S(2)}, u32[]{:S(2)}) %collective-permute-start.7) | collective-permute-done | bytes 524320 | tf_op jit(solution)/shard_map/cond/branch_3_fun/ppermute | solution.py:304
  143.4 1.4 half_sums.1
  144.8 16.1 %conditional.3 = (bf16[512,512]{1,0:T(8,128)(2,1)}, bf16[512,512]{1,0:T(8,128)(2,1)}) conditional(s32[]{:T(128)} %bitcast.1, (bf16[512,512]{1,0:T(8,128)(2,1)S(1)}, bf16[512,512]{1,0:T(8,128)(2,1)S(1)}) %half_sums.1, (bf16[512,512]{1,0:T(8,128)(2,1)S(1)}, bf16[512,512]{1,0:T(8,128)(2,1)S(1)}) %half_sums.1, ...), branch_computations={%region_21.0_spmd, %region_22.0_spmd, %region_23.0_spmd, %region_2... | conditional | bytes 4194400 | solution.py:310
  144.8 0.1 collective-permute-start.48
  144.9 1.1 collective-permute-start.49
  146.0 1.0 collective-permute-done.48
  146.9 13.9 %collective-permute-done.49 = bf16[512,512]{1,0:T(8,128)(2,1)} collective-permute-done((bf16[512,512]{1,0:T(8,128)(2,1)S(1)}, bf16[512,512]{1,0:T(8,128)(2,1)}, u32[]{:S(2)}, u32[]{:S(2)}) %collective-permute-start.49) | collective-permute-done | bytes 524320 | tf_op jit(solution)/shard_map/cond/branch_3_fun/ppermute | solution.py:304
  160.8 3.4 %finish.1 = f32[2,512,512]{2,1,0:T(8,128)} custom-call(s32[2,128]{1,0:T(2,128)S(1)} %copy-done.2, f32[2,512,512]{2,1,0:T(8,128)S(1)} %get-tuple-element.271.own, bf16[512,512]{1,0:T(8,128)(2,1)} %get-tuple-element.275.refs_0_, bf16[512,512]{1,0:T(8,128)(2,1)} %get-tuple-element.276.refs_1_, bf16[512,512]{1,0:T(8,128)(2,1)} %get-tuple-element.277.refs_2_, ...), custom_call_target="tpu_custom_call" | custom-call | tf_op jit(solution)/shard_map/finish/pallas_call | solution.py:279
Async XLA Ops:
  8.0 109.3 %copy-start = (bf16[8,512,512]{2,1,0:T(8,128)(2,1)S(1)}, bf16[8,512,512]{2,1,0:T(8,128)(2,1)}, u32[]{:S(2)}) copy-start(bf16[8,512,512]{2,1,0:T(8,128)(2,1)} %factor_hbm.1) | copy-start | bytes 12582916
  8.0 109.3 %copy-start.1 = (s32[128,128]{1,0:T(8,128)S(1)}, s32[128,128]{1,0:T(8,128)}, u32[]{:S(2)}) copy-start(s32[128,128]{1,0:T(8,128)} %count_hbm.1) | copy-start | bytes 196612
  8.0 109.3 %copy-start.2 = (s32[2,128]{1,0:T(2,128)S(1)}, s32[2,128]{1,0:T(2,128)}, u32[]{:S(2)}) copy-start(s32[2,128]{1,0:T(2,128)} %partners_ref.5) | copy-start | bytes 3076
  127.4 2.1 %collective-permute-start.6 = (bf16[512,512]{1,0:T(8,128)(2,1)S(1)}, bf16[512,512]{1,0:T(8,128)(2,1)}, u32[]{:S(2)}, u32[]{:S(2)}) collective-permute-start(bf16[512,512]{1,0:T(8,128)(2,1)S(1)} %get-tuple-element.179), channel_id=1, source_target_pairs={{0,1},{1,0},{2,3},{3,2},{4,5},{5,4},{6,7},{7,6},{8,9},{9,8},{10,11... | collective-permute-start | bytes 1572872 | tf_op jit(solution)/shard_map/cond/branch_3_fun/ppermute | solution.py:303
  127.5 15.9 %collective-permute-start.7 = (bf16[512,512]{1,0:T(8,128)(2,1)S(1)}, bf16[512,512]{1,0:T(8,128)(2,1)}, u32[]{:S(2)}, u32[]{:S(2)}) collective-permute-start(bf16[512,512]{1,0:T(8,128)(2,1)S(1)} %get-tuple-element.180), channel_id=1, source_target_pairs={{0,16},{1,17},{2,18},{3,19},{4,20},{5,21},{6,22},{7,23},{8,24},{9,... | collective-permute-start | bytes 1572872 | tf_op jit(solution)/shard_map/cond/branch_3_fun/ppermute | solution.py:304
  144.8 2.1 %collective-permute-start.48 = (bf16[512,512]{1,0:T(8,128)(2,1)S(1)}, bf16[512,512]{1,0:T(8,128)(2,1)}, u32[]{:S(2)}, u32[]{:S(2)}) collective-permute-start(bf16[512,512]{1,0:T(8,128)(2,1)S(1)} %get-tuple-element.221), channel_id=1, source_target_pairs={{0,1},{1,0},{2,3},{3,2},{4,5},{5,4},{6,7},{7,6},{8,9},{9,8},{10,11... | collective-permute-start | bytes 1572872 | tf_op jit(solution)/shard_map/cond/branch_3_fun/ppermute | solution.py:303
  144.9 15.9 %collective-permute-start.49 = (bf16[512,512]{1,0:T(8,128)(2,1)S(1)}, bf16[512,512]{1,0:T(8,128)(2,1)}, u32[]{:S(2)}, u32[]{:S(2)}) collective-permute-start(bf16[512,512]{1,0:T(8,128)(2,1)S(1)} %get-tuple-element.222), channel_id=1, source_target_pairs={{0,16},{1,17},{2,18},{3,19},{4,20},{5,21},{6,22},{7,23},{8,24},{9,... | collective-permute-start | bytes 1572872 | tf_op jit(solution)/shard_map/cond/branch_3_fun/ppermute | solution.py:304
